TPU v7x, 32 devices: a whole 2x2x4 slice. The times are simulated.
32 devices in a mesh: phase: 2 (over core), dp: 8 (over z, y), mp: 2 (over x).
Axes of the slice: x: 2, y: 2, z: 4, core: 2. Of those that a mesh axis runs over, the one named last changes fastest.
Arguments:
- segments: bfloat16 [2, 16, 64, 4096], P(None, 'dp', 'mp'), may hold values from -6 to 6
- memory_in: bfloat16 [16, 64, 4096], P('dp', 'mp'), may hold values from -6 to 6
- seg_lengths: int32 [2, 16], P(None, 'dp'), may hold values from 1 to 64, as said below
- routes: int32 [2, 8], replicated, may hold values from 0 to 7, each once within a row
- w_query: bfloat16 [2, 4096, 4096], P('phase', None, 'mp'), may hold values from -12 to 12
- w_key: bfloat16 [2, 4096, 1024], P('phase', None, 'mp'), may hold values from -1 to 1
- value_weight: bfloat16 [2, 4096, 1024], P('phase', None, 'mp'), may hold values from -0.09375 to 0.09375
- w_out: bfloat16 [2, 4096, 4096], P('phase', 'mp'), may hold values from -0.09375 to 0.09375
- norm_gain: bfloat16 [2, 4096], P('phase'), may hold values from 0.099609375 to 1.8984375
Outputs:
- mem_states: bfloat16 [2, 2, 16, 64, 4096], P('phase', None, 'dp', 'mp')
- seg_states: bfloat16 [2, 2, 16, 64, 4096], P('phase', None, 'dp', 'mp')
Inputs may be any that keep to these rules, and one draw needn't show every extreme that they name: Each row m is a permutation of the data groups: slot m of group g hands its memory to slot m of group routes[m, g]. `seg_lengths`: some entry equals 64.
All inputs are finite; a program needn't handle non-finite values.
Results may differ from a plain program's by a relative error of at most 0.025.
Values may be sent and summed in bfloat16 or wider, within the bound.
No kernel may reach another device: no remote copies, remote signals or barrier semaphores. Data moves between devices by JAX's collectives and lax.ppermute only.
A program may use at most 192 MiB of HBM per device.

v0:
```python
import jax
import jax.numpy as jnp
from jax import lax
from jax.sharding import PartitionSpec as P

HEAD_SIZE = 128
EPSILON = 1e-05


def shifted(value, axis, steps):
    count = lax.axis_size(axis)
    pairs = [(source, (source + steps) % count) for source in range(count)]
    return lax.ppermute(value, axis, pairs)


def norm_rows(rows, gain):
    values = rows.astype(jnp.float32)
    scaled = values * lax.rsqrt(jnp.mean(values * values, axis=-1, keepdims=True) + EPSILON)
    return (scaled * gain.astype(jnp.float32)).astype(jnp.bfloat16)


def section_layer(mem_x, seg_x, length, w_query, w_key, value_weight, w_out, gain):
    mem_dev = mem_x.shape[0]
    seg_dev = seg_x.shape[0]
    raw_mem, raw_seg = (
        lax.all_gather(mem_x, "mp", axis=0, tiled=True),
        lax.all_gather(seg_x, "mp", axis=0, tiled=True),
    )
    all_mem = norm_rows(raw_mem, gain)
    all_seg = norm_rows(raw_seg, gain)
    mem_rows = all_mem.shape[0]
    normed = jnp.concatenate([all_mem, all_seg], axis=0)
    rows_total = normed.shape[0]
    kv_dev = w_key.shape[1] // HEAD_SIZE
    query_dev = w_query.shape[1] // HEAD_SIZE
    per_group = query_dev // kv_dev
    heads_of_query = jnp.dot(normed, w_query, preferred_element_type=jnp.float32).astype(
        jnp.bfloat16
    )
    heads_of_query = heads_of_query.reshape(rows_total, kv_dev, per_group, HEAD_SIZE)
    heads_of_key = jnp.dot(normed, w_key, preferred_element_type=jnp.float32).astype(jnp.bfloat16)
    heads_of_key = heads_of_key.reshape(rows_total, kv_dev, HEAD_SIZE)
    heads_of_value = jnp.dot(normed, value_weight, preferred_element_type=jnp.float32).astype(
        jnp.bfloat16
    )
    heads_of_value = heads_of_value.reshape(rows_total, kv_dev, HEAD_SIZE)
    scores = jnp.einsum(
        "qcgd,kcd->cgqk", heads_of_query, heads_of_key, preferred_element_type=jnp.float32
    ) * HEAD_SIZE ** (-0.5)
    query_pos = lax.broadcasted_iota(jnp.int32, (rows_total, rows_total), 0)
    key_pos = lax.broadcasted_iota(jnp.int32, (rows_total, rows_total), 1)
    visible = (key_pos < mem_rows) | (key_pos - mem_rows < length) & (
        (query_pos < mem_rows) | (key_pos <= query_pos)
    )
    scores = jnp.where(visible, scores, -1e30)
    row_max = jnp.max(scores, axis=-1, keepdims=True)
    exponent = jnp.exp(scores - row_max)
    attn = (exponent / jnp.sum(exponent, axis=-1, keepdims=True)).astype(jnp.bfloat16)
    attended = jnp.einsum(
        "cgqk,kcd->qcgd", attn, heads_of_value, preferred_element_type=jnp.float32
    )
    attended = attended.astype(jnp.bfloat16).reshape(rows_total, query_dev * HEAD_SIZE)
    attended_mem = attended[:mem_rows]
    attended_seg = attended[mem_rows:]
    block_rows = mem_dev + seg_dev
    blocks = block_rows * lax.axis_size("mp") // block_rows
    term_mem = jnp.dot(attended_mem, w_out, preferred_element_type=jnp.float32).reshape(
        blocks, mem_dev, -1
    )
    term_seg = jnp.dot(attended_seg, w_out, preferred_element_type=jnp.float32).reshape(
        blocks, seg_dev, -1
    )
    summed = lax.psum_scatter(
        jnp.concatenate([term_mem, term_seg], axis=1)
        .reshape(block_rows * lax.axis_size("mp"), -1)
        .astype(jnp.bfloat16),
        "mp",
        scatter_dimension=0,
        tiled=True,
    ).astype(jnp.float32)
    new_mem = (mem_x.astype(jnp.float32) + summed[:mem_dev]).astype(jnp.bfloat16)
    new_seg = (seg_x.astype(jnp.float32) + summed[mem_dev:]).astype(jnp.bfloat16)
    return (new_mem, new_seg)


def route_memory(arrived, perm_row, group_index):
    group_count = perm_row.shape[0]
    group_ids = jnp.arange(group_count, dtype=jnp.int32)
    target = jnp.sum(jnp.where(group_ids == group_index, perm_row, 0))
    outgoing = jnp.where(
        (group_ids == target)[:, None, None], arrived[None], jnp.zeros_like(arrived)[None]
    )
    received = lax.all_to_all(outgoing, "dp", split_axis=0, concat_axis=0, tiled=True)
    return jnp.sum(received.astype(jnp.float32), axis=0).astype(jnp.bfloat16)


def per_device(
    segments, memory_in, seg_lengths, routes, w_query, w_key, value_weight, w_out, norm_gain
):
    rounds = segments.shape[0]
    slot_count = memory_in.shape[0]
    phase_count = lax.axis_size("phase")
    step_count = rounds * slot_count + phase_count - 1
    phase_index = lax.axis_index("phase")
    group_index = lax.axis_index("dp")
    is_first = phase_index == 0
    items = rounds * slot_count
    lengths_flat = seg_lengths.reshape(items)
    item_ids = jnp.arange(items, dtype=jnp.int32)
    mem_buf = jnp.where(is_first, memory_in[0], jnp.zeros_like(memory_in[0]))
    seg_buf = jnp.where(is_first, segments[0, 0], jnp.zeros_like(segments[0, 0]))
    mem_hist = jnp.zeros((items,) + memory_in.shape[1:], jnp.bfloat16)
    seg_hist = jnp.zeros((items,) + segments.shape[2:], jnp.bfloat16)
    for step in range(step_count):
        item_index = step - phase_index
        is_valid = (item_index >= 0) & (item_index < items)
        clipped = jnp.clip(item_index, 0, items - 1)
        length = jnp.sum(jnp.where(item_ids == clipped, lengths_flat, 0))
        mem_new, seg_new = section_layer(
            mem_buf, seg_buf, length, w_query[0], w_key[0], value_weight[0], w_out[0], norm_gain[0]
        )
        mem_current = lax.dynamic_index_in_dim(mem_hist, clipped, 0, keepdims=False)
        seg_current = lax.dynamic_index_in_dim(seg_hist, clipped, 0, keepdims=False)
        mem_hist = lax.dynamic_update_index_in_dim(
            mem_hist, jnp.where(is_valid, mem_new, mem_current), clipped, 0
        )
        seg_hist = lax.dynamic_update_index_in_dim(
            seg_hist, jnp.where(is_valid, seg_new, seg_current), clipped, 0
        )
        if step + 1 < step_count:
            mem_pass, seg_pass = shifted((mem_new, seg_new), "phase", 1)
            next_item = step + 1
            if next_item < items:
                next_round, next_slot = divmod(next_item, slot_count)
                if next_round == 0:
                    first_mem = memory_in[next_slot]
                else:
                    first_mem = route_memory(mem_pass, routes[next_slot], group_index)
                first_seg = segments[next_round, next_slot]
            else:
                first_mem = jnp.zeros_like(mem_pass)
                first_seg = jnp.zeros_like(seg_pass)
            mem_buf = jnp.where(is_first, first_mem, mem_pass)
            seg_buf = jnp.where(is_first, first_seg, seg_pass)
    mem_states = mem_hist.reshape((1, rounds, slot_count) + memory_in.shape[1:])
    seg_states = seg_hist.reshape((1, rounds, slot_count) + segments.shape[2:])
    return (mem_states, seg_states)


def solution(mesh):
    return jax.shard_map(
        per_device,
        mesh=mesh,
        in_specs=(
            P(None, "dp", "mp", None),
            P("dp", "mp", None),
            P(None, "dp"),
            P(),
            P("phase", None, "mp"),
            P("phase", None, "mp"),
            P("phase", None, "mp"),
            P("phase", "mp", None),
            P("phase", None),
        ),
        out_specs=(P("phase", None, "dp", "mp", None), P("phase", None, "dp", "mp", None)),
        check_vma=False,
    )
```

profile of v0, /device:TPU:0, one launch (start us, length us, event | category | flops | bytes accessed | tf_op | source)
XLA Modules:
  0.0 495.5 jit_solution(5529236552270811867)
XLA Ops:
  7.3 1.6 fusion.256
  13.1 9.9 %all-gather.1 = bf16[1,1,64,4096]{3,2,1,0:T(8,128)(2,1)S(1)} all-gather(bf16[1,1,32,4096]{3,2,1,0:T(8,128)(2,1)S(1)} %slice_select_fusion), channel_id=3, replica_groups=mesh['phase'=2,'dp'=8,'mp'=2] {'mp'}, dimensions={2}, use_global_device_ids=true | all-gather | bytes 786432 | tf_op jit(solution)/shard_map/all_gather | solution.py:27
  24.2 8.1 %all-gather = bf16[1,64,4096]{2,1,0:T(8,128)(2,1)S(1)} all-gather(bf16[1,32,4096]{2,1,0:T(8,128)(2,1)S(1)} %slice_select_fusion.1), channel_id=2, replica_groups=mesh['phase'=2,'dp'=8,'mp'=2] {'mp'}, dimensions={1}, use_global_device_ids=true | all-gather | bytes 786432 | tf_op jit(solution)/shard_map/all_gather | solution.py:26
  34.5 8.1 %fusion.85 = bf16[128,2048]{1,0:T(8,128)(2,1)S(1)} fusion(bf16[1,4096,2048]{2,1,0:T(8,128)(2,1)} %param.13, bf16[64,4096]{1,0:T(8,128)(2,1)S(1)} %get-tuple-element.52, bf16[64,4096]{1,0:T(8,128)(2,1)S(1)} %get-tuple-element.51), kind=kOutput, calls=%fused_computation.65 | convolution fusion | flops 2149842944 | bytes 18350080 | tf_op jit(solution)/shard_map/dot_general | solution.py:37
  44.6 2.9 fusion.125
  48.8 8.8 %fusion.35 = bf16[2,32,4096]{2,1,0:T(8,128)(2,1)S(1)} fusion(bf16[2,32,2048]{2,1,0:T(8,128)(2,1)S(1)} %dot_general.130, bf16[1,2048,4096]{2,1,0:T(8,128)(2,1)} %param.16), kind=kOutput, calls=%fused_computation.35 | convolution fusion | flops 1074003968 | bytes 17563648 | tf_op jit(solution)/shard_map/dot_general | solution.py:67
  57.6 8.8 %fusion.38 = bf16[2,32,4096]{2,1,0:T(8,128)(2,1)S(1)} fusion(bf16[2,32,2048]{2,1,0:T(8,128)(2,1)S(1)} %dot_general.132, bf16[1,2048,4096]{2,1,0:T(8,128)(2,1)} %param.16), kind=kOutput, calls=%fused_computation.36 | convolution fusion | flops 1074003968 | bytes 17563648 | tf_op jit(solution)/shard_map/dot_general | solution.py:70
  66.4 1.0 pad_maximum_fusion.1
  67.5 9.4 %reduce-scatter.8.cloned.1.call-start = ((), (), s32[]{:S(2)}) async-start(), calls=%async_computation.8 | async-start | bytes 1572864 | tf_op jit(solution)/shard_map/reduce_scatter | solution.py:73
  77.0 12.3 %reduce-scatter.6.cloned.1.call-done = bf16[64,4096]{1,0:T(8,128)(2,1)} async-done(((bf16[128,4096]{1,0:T(8,128)(2,1)}), bf16[64,4096]{1,0:T(8,128)(2,1)}) %reduce-scatter.6.cloned.1.call-update) | async-done | bytes 524304 | tf_op jit(solution)/shard_map/reduce_scatter | solution.py:73
  89.3 1.1 convert_element_type.272
  90.8 1.2 bitcast_dynamic-update-slice_fusion.3
  92.7 8.9 %all_gather.32 = bf16[64,4096]{1,0:T(8,128)(2,1)S(1)} all-gather(bf16[32,4096]{1,0:T(8,128)(2,1)S(1)} %bitcast_select_fusion.9), channel_id=1, replica_groups=mesh['phase'=2,'dp'=8,'mp'=2] {'mp'}, dimensions={0}, use_global_device_ids=true | all-gather | bytes 786432 | tf_op jit(solution)/shard_map/all_gather | solution.py:26
  101.8 1.0 bitcast_select_fusion.8
  102.8 8.0 %all_gather.33 = bf16[64,4096]{1,0:T(8,128)(2,1)S(1)} all-gather(bf16[32,4096]{1,0:T(8,128)(2,1)S(1)} %bitcast_select_fusion.8), channel_id=1, replica_groups=mesh['phase'=2,'dp'=8,'mp'=2] {'mp'}, dimensions={0}, use_global_device_ids=true | all-gather | bytes 786432 | tf_op jit(solution)/shard_map/all_gather | solution.py:27
  112.2 8.3 %fusion.88 = bf16[128,2048]{1,0:T(8,128)(2,1)S(1)} fusion(bf16[1,4096,2048]{2,1,0:T(8,128)(2,1)} %param.13, bf16[64,4096]{1,0:T(8,128)(2,1)S(1)} %get-tuple-element.50, bf16[64,4096]{1,0:T(8,128)(2,1)S(1)} %get-tuple-element.49), kind=kOutput, calls=%fused_computation.66 | convolution fusion | flops 2149842944 | bytes 18350080 | tf_op jit(solution)/shard_map/dot_general | solution.py:37
  121.3 1.2 reshape.227
  122.5 2.3 fusion.117
  124.8 1.5 fusion.307
  126.4 2.0 fusion.121
  129.5 8.8 %fusion.41 = bf16[2,32,4096]{2,1,0:T(8,128)(2,1)S(1)} fusion(bf16[2,32,2048]{2,1,0:T(8,128)(2,1)S(1)} %dot_general.139, bf16[1,2048,4096]{2,1,0:T(8,128)(2,1)} %param.16), kind=kOutput, calls=%fused_computation.37 | convolution fusion | flops 1074003968 | bytes 17563648 | tf_op jit(solution)/shard_map/dot_general | solution.py:67
  139.3 1.1 dot_general.141
  140.4 8.8 %fusion.44 = bf16[2,32,4096]{2,1,0:T(8,128)(2,1)S(1)} fusion(bf16[2,32,2048]{2,1,0:T(8,128)(2,1)S(1)} %dot_general.141, bf16[1,2048,4096]{2,1,0:T(8,128)(2,1)} %param.16), kind=kOutput, calls=%fused_computation.38 | convolution fusion | flops 1074003968 | bytes 17563648 | tf_op jit(solution)/shard_map/dot_general | solution.py:70
  149.2 1.0 pad_maximum_fusion.3
  150.4 20.5 %reduce-scatter.8.cloned.1.call-done = bf16[64,4096]{1,0:T(8,128)(2,1)} async-done(((bf16[128,4096]{1,0:T(8,128)(2,1)}), bf16[64,4096]{1,0:T(8,128)(2,1)}) %reduce-scatter.8.cloned.1.call-update) | async-done | bytes 524304 | tf_op jit(solution)/shard_map/reduce_scatter | solution.py:73
  170.8 1.1 convert_element_type.288
  174.6 1.6 broadcast_select_fusion.1
  176.2 5.5 %all-to-all-start = ((bf16[8,32,4096]{2,1,0:T(8,128)(2,1)}), bf16[8,32,4096]{2,1,0:T(8,128)(2,1)S(1)}, u32[]{:S(2)}, u32[]{:S(2)}) async-start(bf16[8,32,4096]{2,1,0:T(8,128)(2,1)} %broadcast_select_fusion.1), calls=%async_computation.2 | async-start | bytes 4194304 | tf_op jit(solution)/shard_map/all_to_all | solution.py:93
  181.9 1.5 collective-permute-done.3
  184.4 9.0 %all_gather.35 = bf16[64,4096]{1,0:T(8,128)(2,1)S(1)} all-gather(bf16[32,4096]{1,0:T(8,128)(2,1)S(1)} %bitcast_select_fusion.6), channel_id=1, replica_groups=mesh['phase'=2,'dp'=8,'mp'=2] {'mp'}, dimensions={0}, use_global_device_ids=true | all-gather | bytes 786432 | tf_op jit(solution)/shard_map/all_gather | solution.py:27
  193.6 36.7 %all-to-all-done = bf16[8,32,4096]{2,1,0:T(8,128)(2,1)S(1)} async-done(((bf16[8,32,4096]{2,1,0:T(8,128)(2,1)}), bf16[8,32,4096]{2,1,0:T(8,128)(2,1)S(1)}, u32[]{:S(2)}, u32[]{:S(2)}) %all-to-all-start) | async-done | bytes 2097184 | tf_op jit(solution)/shard_map/all_to_all | solution.py:93
  230.7 8.1 %all_gather.34 = bf16[64,4096]{1,0:T(8,128)(2,1)S(1)} all-gather(bf16[32,4096]{1,0:T(8,128)(2,1)S(1)} %broadcast_select_fusion.5), channel_id=1, replica_groups=mesh['phase'=2,'dp'=8,'mp'=2] {'mp'}, dimensions={0}, use_global_device_ids=true | all-gather | bytes 786432 | tf_op jit(solution)/shard_map/all_gather | solution.py:26
  240.2 8.3 %fusion.91 = bf16[128,2048]{1,0:T(8,128)(2,1)S(1)} fusion(bf16[1,4096,2048]{2,1,0:T(8,128)(2,1)} %param.13, bf16[64,4096]{1,0:T(8,128)(2,1)S(1)} %get-tuple-element.48, bf16[64,4096]{1,0:T(8,128)(2,1)S(1)} %get-tuple-element.47), kind=kOutput, calls=%fused_computation.67 | convolution fusion | flops 2149842944 | bytes 18350080 | tf_op jit(solution)/shard_map/dot_general | solution.py:37
  251.4 8.8 %fusion.47 = bf16[2,32,4096]{2,1,0:T(8,128)(2,1)S(1)} fusion(bf16[2,32,2048]{2,1,0:T(8,128)(2,1)S(1)} %dot_general.148, bf16[1,2048,4096]{2,1,0:T(8,128)(2,1)} %param.16), kind=kOutput, calls=%fused_computation.39 | convolution fusion | flops 1074003968 | bytes 17563648 | tf_op jit(solution)/shard_map/dot_general | solution.py:67
  260.6 8.8 %fusion.50 = bf16[2,32,4096]{2,1,0:T(8,128)(2,1)S(1)} fusion(bf16[2,32,2048]{2,1,0:T(8,128)(2,1)S(1)} %dot_general.150, bf16[1,2048,4096]{2,1,0:T(8,128)(2,1)} %param.16), kind=kOutput, calls=%fused_computation.40 | convolution fusion | flops 1074003968 | bytes 17563648 | tf_op jit(solution)/shard_map/dot_general | solution.py:70
  269.4 1.0 pad_maximum_fusion.5
  272.4 17.6 %reduce-scatter.10.cloned.1.call-done = bf16[64,4096]{1,0:T(8,128)(2,1)} async-done(((bf16[128,4096]{1,0:T(8,128)(2,1)}), bf16[64,4096]{1,0:T(8,128)(2,1)}) %reduce-scatter.10.cloned.1.call-update) | async-done | bytes 524304 | tf_op jit(solution)/shard_map/reduce_scatter | solution.py:73
  290.0 1.1 convert_element_type.304
  291.1 1.0 bitcast_dynamic-update-slice_fusion.1
  293.7 1.6 broadcast_select_fusion
  295.3 5.5 %all-to-all-start.1 = ((bf16[8,32,4096]{2,1,0:T(8,128)(2,1)}), bf16[8,32,4096]{2,1,0:T(8,128)(2,1)S(1)}, u32[]{:S(2)}, u32[]{:S(2)}) async-start(bf16[8,32,4096]{2,1,0:T(8,128)(2,1)} %broadcast_select_fusion), calls=%async_computation.4 | async-start | bytes 4194304 | tf_op jit(solution)/shard_map/all_to_all | solution.py:93
  301.1 1.5 collective-permute-done.5
  303.6 9.0 %all_gather.37 = bf16[64,4096]{1,0:T(8,128)(2,1)S(1)} all-gather(bf16[32,4096]{1,0:T(8,128)(2,1)S(1)} %bitcast_select_fusion.4), channel_id=1, replica_groups=mesh['phase'=2,'dp'=8,'mp'=2] {'mp'}, dimensions={0}, use_global_device_ids=true | all-gather | bytes 786432 | tf_op jit(solution)/shard_map/all_gather | solution.py:27
  312.8 36.5 %all-to-all-done.1 = bf16[8,32,4096]{2,1,0:T(8,128)(2,1)S(1)} async-done(((bf16[8,32,4096]{2,1,0:T(8,128)(2,1)}), bf16[8,32,4096]{2,1,0:T(8,128)(2,1)S(1)}, u32[]{:S(2)}, u32[]{:S(2)}) %all-to-all-start.1) | async-done | bytes 2097184 | tf_op jit(solution)/shard_map/all_to_all | solution.py:93
  349.3 1.1 reduce_sum.237
  350.4 1.1 broadcast_select_fusion.4
  351.5 7.2 %all_gather.36 = bf16[64,4096]{1,0:T(8,128)(2,1)S(1)} all-gather(bf16[32,4096]{1,0:T(8,128)(2,1)S(1)} %broadcast_select_fusion.4), channel_id=1, replica_groups=mesh['phase'=2,'dp'=8,'mp'=2] {'mp'}, dimensions={0}, use_global_device_ids=true | all-gather | bytes 786432 | tf_op jit(solution)/shard_map/all_gather | solution.py:26
  360.0 8.3 %fusion.94 = bf16[128,2048]{1,0:T(8,128)(2,1)S(1)} fusion(bf16[1,4096,2048]{2,1,0:T(8,128)(2,1)} %param.13, bf16[64,4096]{1,0:T(8,128)(2,1)S(1)} %get-tuple-element.46, bf16[64,4096]{1,0:T(8,128)(2,1)S(1)} %get-tuple-element.45), kind=kOutput, calls=%fused_computation.68 | convolution fusion | flops 2149842944 | bytes 18350080 | tf_op jit(solution)/shard_map/dot_general | solution.py:37
  371.2 8.8 %fusion.53 = bf16[2,32,4096]{2,1,0:T(8,128)(2,1)S(1)} fusion(bf16[2,32,2048]{2,1,0:T(8,128)(2,1)S(1)} %dot_general.157, bf16[1,2048,4096]{2,1,0:T(8,128)(2,1)} %param.16), kind=kOutput, calls=%fused_computation.41 | convolution fusion | flops 1074003968 | bytes 17563648 | tf_op jit(solution)/shard_map/dot_general | solution.py:67
  380.5 8.9 %fusion.56 = bf16[2,32,4096]{2,1,0:T(8,128)(2,1)S(1)} fusion(bf16[2,32,2048]{2,1,0:T(8,128)(2,1)S(1)} %dot_general.159, bf16[1,2048,4096]{2,1,0:T(8,128)(2,1)} %param.16), kind=kOutput, calls=%fused_computation.42 | convolution fusion | flops 1074003968 | bytes 17563648 | tf_op jit(solution)/shard_map/dot_general | solution.py:70
  389.4 1.0 pad_maximum_fusion.7
  390.6 19.3 %reduce-scatter.12.cloned.1.call-done = bf16[64,4096]{1,0:T(8,128)(2,1)} async-done(((bf16[128,4096]{1,0:T(8,128)(2,1)}), bf16[64,4096]{1,0:T(8,128)(2,1)}) %reduce-scatter.12.cloned.1.call-update) | async-done | bytes 524304 | tf_op jit(solution)/shard_map/reduce_scatter | solution.py:73
  409.9 1.1 convert_element_type.320
  411.8 1.0 collective-permute-done.7
  413.6 9.2 %all_gather.39 = bf16[64,4096]{1,0:T(8,128)(2,1)S(1)} all-gather(bf16[32,4096]{1,0:T(8,128)(2,1)S(1)} %broadcast_select_fusion.2), channel_id=1, replica_groups=mesh['phase'=2,'dp'=8,'mp'=2] {'mp'}, dimensions={0}, use_global_device_ids=true | all-gather | bytes 786432 | tf_op jit(solution)/shard_map/all_gather | solution.py:27
  423.1 8.2 %all_gather.38 = bf16[64,4096]{1,0:T(8,128)(2,1)S(1)} all-gather(bf16[32,4096]{1,0:T(8,128)(2,1)S(1)} %broadcast_select_fusion.3), channel_id=1, replica_groups=mesh['phase'=2,'dp'=8,'mp'=2] {'mp'}, dimensions={0}, use_global_device_ids=true | all-gather | bytes 786432 | tf_op jit(solution)/shard_map/all_gather | solution.py:26
  432.6 8.3 %fusion.97 = bf16[128,2048]{1,0:T(8,128)(2,1)S(1)} fusion(bf16[1,4096,2048]{2,1,0:T(8,128)(2,1)} %param.13, bf16[64,4096]{1,0:T(8,128)(2,1)S(1)} %get-tuple-element.44, bf16[64,4096]{1,0:T(8,128)(2,1)S(1)} %get-tuple-element.43), kind=kOutput, calls=%fused_computation.69 | convolution fusion | flops 2149842944 | bytes 18350080 | tf_op jit(solution)/shard_map/dot_general | solution.py:37
  442.1 1.3 fusion.111
  443.9 2.0 fusion.124
  446.3 8.8 %fusion.59 = bf16[2,32,4096]{2,1,0:T(8,128)(2,1)S(1)} fusion(bf16[2,32,2048]{2,1,0:T(8,128)(2,1)S(1)} %dot_general.166, bf16[1,2048,4096]{2,1,0:T(8,128)(2,1)} %param.16), kind=kOutput, calls=%fused_computation.43 | convolution fusion | flops 1074003968 | bytes 17563648 | tf_op jit(solution)/shard_map/dot_general | solution.py:67
  455.5 8.8 %fusion.62 = bf16[2,32,4096]{2,1,0:T(8,128)(2,1)S(1)} fusion(bf16[2,32,2048]{2,1,0:T(8,128)(2,1)S(1)} %dot_general.168, bf16[1,2048,4096]{2,1,0:T(8,128)(2,1)} %param.16), kind=kOutput, calls=%fused_computation.44 | convolution fusion | flops 1074003968 | bytes 17563648 | tf_op jit(solution)/shard_map/dot_general | solution.py:70
  464.4 1.0 pad_maximum_fusion.9
  465.5 20.5 %reduce-scatter.14.cloned.1.call-done = bf16[64,4096]{1,0:T(8,128)(2,1)} async-done(((bf16[128,4096]{1,0:T(8,128)(2,1)}), bf16[64,4096]{1,0:T(8,128)(2,1)}) %reduce-scatter.14.cloned.1.call-update) | async-done | bytes 524304 | tf_op jit(solution)/shard_map/reduce_scatter | solution.py:73
  486.0 1.1 convert_element_type.336
  (187 shorter events, 42.1 us)
Async XLA Ops:
  7.2 82.1 %reduce-scatter.6.cloned.1.call-start = ((), (), s32[]{:S(2)}) async-start(), calls=%async_computation.7 | async-start | bytes 1572864 | tf_op jit(solution)/shard_map/reduce_scatter | solution.py:73
  7.2 26.4 %copy-start.16 = (bf16[1,4096,512]{2,1,0:T(8,128)(2,1)S(1)}, bf16[1,4096,512]{2,1,0:T(8,128)(2,1)}, u32[]{:S(2)}) copy-start(bf16[1,4096,512]{2,1,0:T(8,128)(2,1)} %param.14) | copy-start | bytes 12582916
  66.4 24.1 %copy-start.6 = (bf16[2,32,4096]{2,1,0:T(8,128)(2,1)S(1)}, bf16[2,32,4096]{2,1,0:T(8,128)(2,1)}, u32[]{:S(2)}) copy-start(bf16[2,32,4096]{2,1,0:T(8,128)(2,1)} %param.10) | copy-start | bytes 1572868
  67.5 103.3 %reduce-scatter.8.cloned.1.call-start = ((), (), s32[]{:S(2)}) async-start(), calls=%async_computation.8 | async-start | bytes 1572864 | tf_op jit(solution)/shard_map/reduce_scatter | solution.py:73
  90.6 20.8 %copy-start.17 = (bf16[1,4096,512]{2,1,0:T(8,128)(2,1)S(1)}, bf16[1,4096,512]{2,1,0:T(8,128)(2,1)}, u32[]{:S(2)}) copy-start(bf16[1,4096,512]{2,1,0:T(8,128)(2,1)} %param.14) | copy-start | bytes 12582916
  90.6 2.0 collective-permute-start
  92.0 9.8 %collective-permute-start.1 = (bf16[32,4096]{1,0:T(8,128)(2,1)S(1)}, bf16[32,4096]{1,0:T(8,128)(2,1)S(1)}, u32[]{:S(2)}, u32[]{:S(2)}) collective-permute-start(bf16[32,4096]{1,0:T(8,128)(2,1)S(1)} %get-tuple-element.16), channel_id=1, source_target_pairs={{0,16},{16,0},{1,17},{17,1},{2,18},{18,2},{3,19},{19,3},{4,20},{20... | collective-permute-start | bytes 786440 | tf_op jit(solution)/shard_map/ppermute | solution.py:13
  112.2 8.4 %copy-start.21 = (bf16[1,4096,512]{2,1,0:T(8,128)(2,1)S(1)}, bf16[1,4096,512]{2,1,0:T(8,128)(2,1)}, u32[]{:S(2)}) copy-start(bf16[1,4096,512]{2,1,0:T(8,128)(2,1)} %param.15) | copy-start | bytes 12582916
  129.5 8.9 %copy-start.7 = (bf16[64,4,4,128]{3,0,2,1:T(8,128)(2,1)S(1)}, bf16[64,4,4,128]{3,0,2,1:T(8,128)(2,1)}, u32[]{:S(2)}) copy-start(bf16[64,4,4,128]{3,0,2,1:T(8,128)(2,1)} %get-tuple-element.40) | copy-start | bytes 786436
  149.2 23.7 %copy-start.15 = (s32[2,8]{1,0:T(2,128)S(1)}, s32[2,8]{1,0:T(2,128)}, u32[]{:S(2)}) copy-start(s32[2,8]{1,0:T(2,128)} %param.12) | copy-start | bytes 196
  172.9 3.3 copy-start
  172.9 3.3 copy-start.3
  172.9 1.7 collective-permute-start.2
  176.2 54.1 %all-to-all-start = ((bf16[8,32,4096]{2,1,0:T(8,128)(2,1)}), bf16[8,32,4096]{2,1,0:T(8,128)(2,1)S(1)}, u32[]{:S(2)}, u32[]{:S(2)}) async-start(bf16[8,32,4096]{2,1,0:T(8,128)(2,1)} %broadcast_select_fusion.1), calls=%async_computation.2 | async-start | bytes 4194304 | tf_op jit(solution)/shard_map/all_to_all | solution.py:93
  181.7 108.3 %reduce-scatter.10.cloned.1.call-start = ((), (), s32[]{:S(2)}) async-start(), calls=%async_computation.9 | async-start | bytes 1572864 | tf_op jit(solution)/shard_map/reduce_scatter | solution.py:73
  181.8 1.6 collective-permute-start.3
  230.7 8.7 %copy-start.18 = (bf16[1,4096,512]{2,1,0:T(8,128)(2,1)S(1)}, bf16[1,4096,512]{2,1,0:T(8,128)(2,1)}, u32[]{:S(2)}) copy-start(bf16[1,4096,512]{2,1,0:T(8,128)(2,1)} %param.14) | copy-start | bytes 12582916
  240.2 8.3 %copy-start.22 = (bf16[1,4096,512]{2,1,0:T(8,128)(2,1)S(1)}, bf16[1,4096,512]{2,1,0:T(8,128)(2,1)}, u32[]{:S(2)}) copy-start(bf16[1,4096,512]{2,1,0:T(8,128)(2,1)} %param.15) | copy-start | bytes 12582916
  248.5 1.1 copy-start.14
  292.2 1.5 collective-permute-start.4
  295.3 54.0 %all-to-all-start.1 = ((bf16[8,32,4096]{2,1,0:T(8,128)(2,1)}), bf16[8,32,4096]{2,1,0:T(8,128)(2,1)S(1)}, u32[]{:S(2)}, u32[]{:S(2)}) async-start(bf16[8,32,4096]{2,1,0:T(8,128)(2,1)} %broadcast_select_fusion), calls=%async_computation.4 | async-start | bytes 4194304 | tf_op jit(solution)/shard_map/all_to_all | solution.py:93
  300.8 109.1 %reduce-scatter.12.cloned.1.call-start = ((), (), s32[]{:S(2)}) async-start(), calls=%async_computation.10 | async-start | bytes 1572864 | tf_op jit(solution)/shard_map/reduce_scatter | solution.py:73
  301.0 1.6 collective-permute-start.5
  350.4 8.9 %copy-start.19 = (bf16[1,4096,512]{2,1,0:T(8,128)(2,1)S(1)}, bf16[1,4096,512]{2,1,0:T(8,128)(2,1)}, u32[]{:S(2)}) copy-start(bf16[1,4096,512]{2,1,0:T(8,128)(2,1)} %param.14) | copy-start | bytes 12582916
  360.0 8.3 %copy-start.23 = (bf16[1,4096,512]{2,1,0:T(8,128)(2,1)S(1)}, bf16[1,4096,512]{2,1,0:T(8,128)(2,1)}, u32[]{:S(2)}) copy-start(bf16[1,4096,512]{2,1,0:T(8,128)(2,1)} %param.15) | copy-start | bytes 12582916
  368.3 1.1 copy-start.13
  380.4 10.1 %copy-start.4 = (bf16[4,32,4096]{2,1,0:T(8,128)(2,1)S(1)}, bf16[4,32,4096]{2,1,0:T(8,128)(2,1)}, u32[]{:S(2)}) copy-start(bf16[4,32,4096]{2,1,0:T(8,128)(2,1)} %get-tuple-element.29) | copy-start | bytes 3145732
  380.4 10.1 %copy-start.1 = (bf16[4,32,4096]{2,1,0:T(8,128)(2,1)S(1)}, bf16[4,32,4096]{2,1,0:T(8,128)(2,1)}, u32[]{:S(2)}) copy-start(bf16[4,32,4096]{2,1,0:T(8,128)(2,1)} %get-tuple-element.11) | copy-start | bytes 3145732
  390.5 95.5 %reduce-scatter.14.cloned.1.call-start = ((), (), s32[]{:S(2)}) async-start(), calls=%async_computation.11 | async-start | bytes 1572864 | tf_op jit(solution)/shard_map/reduce_scatter | solution.py:73
  411.0 20.8 %copy-start.20 = (bf16[1,4096,512]{2,1,0:T(8,128)(2,1)S(1)}, bf16[1,4096,512]{2,1,0:T(8,128)(2,1)}, u32[]{:S(2)}) copy-start(bf16[1,4096,512]{2,1,0:T(8,128)(2,1)} %param.14) | copy-start | bytes 12582916
  411.2 1.6 collective-permute-start.7
  411.3 11.7 %collective-permute-start.6 = (bf16[32,4096]{1,0:T(8,128)(2,1)S(1)}, bf16[32,4096]{1,0:T(8,128)(2,1)S(1)}, u32[]{:S(2)}, u32[]{:S(2)}) collective-permute-start(bf16[32,4096]{1,0:T(8,128)(2,1)S(1)} %get-tuple-element.28), channel_id=1, source_target_pairs={{0,16},{16,0},{1,17},{17,1},{2,18},{18,2},{3,19},{19,3},{4,20},{20... | collective-permute-start | bytes 786440 | tf_op jit(solution)/shard_map/ppermute | solution.py:13
  412.8 0.7 copy-start.8
  423.0 8.4 %copy-start.10 = (bf16[32,4096]{1,0:T(8,128)(2,1)}, bf16[32,4096]{1,0:T(8,128)(2,1)S(1)}, u32[]{:S(2)}) copy-start(bf16[32,4096]{1,0:T(8,128)(2,1)S(1)} %collective-permute-done.6) | copy-start | bytes 786436
  432.6 8.4 %copy-start.24 = (bf16[1,4096,512]{2,1,0:T(8,128)(2,1)S(1)}, bf16[1,4096,512]{2,1,0:T(8,128)(2,1)}, u32[]{:S(2)}) copy-start(bf16[1,4096,512]{2,1,0:T(8,128)(2,1)} %param.15) | copy-start | bytes 12582916
  440.9 1.1 copy-start.12
  464.3 22.7 %copy-start.9 = (bf16[32,4096]{1,0:T(8,128)(2,1)S(1)}, bf16[32,4096]{1,0:T(8,128)(2,1)}, u32[]{:S(2)}) copy-start(bf16[32,4096]{1,0:T(8,128)(2,1)} %copy-done.8) | copy-start | bytes 786436
  464.3 22.7 %copy-start.11 = (bf16[32,4096]{1,0:T(8,128)(2,1)S(1)}, bf16[32,4096]{1,0:T(8,128)(2,1)}, u32[]{:S(2)}) copy-start(bf16[32,4096]{1,0:T(8,128)(2,1)} %copy-done.10) | copy-start | bytes 786436
  487.3 1.0 copy-start.2
  487.3 1.3 copy-start.5
Sparse Core Ops, SparseCore 0:
  67.6 21.6 reduce-scatter.5
  150.4 20.3 reduce-scatter.7
  270.6 19.4 reduce-scatter.9
  390.6 19.2 reduce-scatter.11
  465.5 20.3 reduce-scatter.13
where the time goes:
time: 505 us; the launch traced here: 496 us
  waiting for transfers between devices  169 us (33%)
  matrix products  152 us (30%)
  blocking collectives  85.7 us (17%)
  other arithmetic  37.4 us (7%)
  starting transfers between devices  22.2 us (4%)
  between operations  15.3 us (3%)
  local copies, waits for them, and re-layouts  13.8 us (3%)
    reduce_scatter x5, waiting for transfers between devices, section_layer(): lax.psum_scatter(jnp.concatenate([term_mem, term_seg], axis=1).reshape(bl...  90.2 us
    all_to_all x2, waiting for transfers between devices, route_memory(): lax.all_to_all(outgoing, 'dp', split_axis=0, concat_axis=0, tiled=True)  73.2 us
    all_gather x5, blocking collectives, section_layer(): lax.all_gather(seg_x, 'mp', axis=0, tiled=True)  45.2 us
    dot_general x5, matrix products, section_layer(): jnp.dot(attended_seg, w_out, preferred_element_type=jnp.float32)  44.1 us
    dot_general x5, matrix products, section_layer(): jnp.dot(attended_mem, w_out, preferred_element_type=jnp.float32)  44 us
    dot_general x5, matrix products, section_layer(): jnp.dot(normed, w_query, preferred_element_type=jnp.float32)  41.3 us
    all_gather x5, blocking collectives, section_layer(): lax.all_gather(mem_x, 'mp', axis=0, tiled=True)  40.5 us
    all_to_all x2, starting transfers between devices, route_memory(): lax.all_to_all(outgoing, 'dp', split_axis=0, concat_axis=0, tiled=True)  11 us
  transfers between devices with their start and end apart: 15, of which 12 were waited for; matrix products, arithmetic and copies ran while one was open for 2% of the time, Pallas kernels for 0%

commit v1 on v0

--- a/solution.py
+++ b/solution.py
@@ -5,6 +5,18 @@
 
 HEAD_SIZE = 128
 EPSILON = 1e-05
+
+
+def collect(x, axis, dim):
+    ways, here = (lax.axis_size(axis), lax.axis_index(axis))
+    grown, reach = (x, 1)
+    while reach < ways:
+        theirs = lax.ppermute(grown, axis, [(d, d ^ reach) for d in range(ways)])
+        mine_first = jnp.concatenate([grown, theirs], axis=dim)
+        theirs_first = jnp.concatenate([theirs, grown], axis=dim)
+        grown = jnp.where(here & reach == 0, mine_first, theirs_first)
+        reach = 2 * reach
+    return grown
 
 
 def shifted(value, axis, steps):
@@ -22,10 +34,7 @@
 def section_layer(mem_x, seg_x, length, w_query, w_key, value_weight, w_out, gain):
     mem_dev = mem_x.shape[0]
     seg_dev = seg_x.shape[0]
-    raw_mem, raw_seg = (
-        lax.all_gather(mem_x, "mp", axis=0, tiled=True),
-        lax.all_gather(seg_x, "mp", axis=0, tiled=True),
-    )
+    raw_mem, raw_seg = (lax.all_gather(mem_x, "mp", axis=0, tiled=True), collect(seg_x, "mp", 0))
     all_mem = norm_rows(raw_mem, gain)
     all_seg = norm_rows(raw_seg, gain)
     mem_rows = all_mem.shape[0]

time: 505 us -> 521 us (1.032)
  blocking collectives: 85.7 us -> 45.2 us
  waiting for transfers between devices: 169 us -> 197 us
  local copies, waits for them, and re-layouts: 13.8 us -> 24.3 us
  matrix products: 152 us -> 159 us
  other arithmetic: 37.4 us -> 43.3 us
    all_gather x5 -> x0, blocking collectives: 45.2 us -> none  [section_layer(): lax.all_gather(seg_x, 'mp', axis=0, tiled=True)]
    ppermute x0 -> x5, waiting for transfers between devices: none -> 29.3 us  [collect(): theirs = lax.ppermute(grown, axis, [(d, d ^ reach) for d in range(ways)])]
    unnamed x50 -> x54, local copies, waits for them, and re-layouts: 2.12 us -> 9.56 us
  transfers between devices with their start and end apart: 15 -> 20, of which waited for: 12 -> 15; matrix products, arithmetic and copies ran while one was open for 2% -> 3% of each run, Pallas kernels for 0% -> 0%
where the time goes in v1:
time: 521 us; the launch traced here: 511 us
  waiting for transfers between devices  197 us (38%)
  matrix products  159 us (31%)
  blocking collectives  45.2 us (9%)
  other arithmetic  43.3 us (8%)
  starting transfers between devices  27.1 us (5%)
  local copies, waits for them, and re-layouts  24.3 us (5%)
  between operations  15.1 us (3%)
    reduce_scatter x5, waiting for transfers between devices, section_layer(): lax.psum_scatter(jnp.concatenate([term_mem, term_seg], axis=1).reshape(bl...  89.4 us
    all_to_all x2, waiting for transfers between devices, route_memory(): lax.all_to_all(outgoing, 'dp', split_axis=0, concat_axis=0, tiled=True)  73.8 us
    all_gather x5, blocking collectives, section_layer(): lax.all_gather(mem_x, 'mp', axis=0, tiled=True)  45.2 us
    dot_general x5, matrix products, section_layer(): jnp.dot(attended_mem, w_out, preferred_element_type=jnp.float32)  44.1 us
    dot_general x5, matrix products, section_layer(): jnp.dot(attended_seg, w_out, preferred_element_type=jnp.float32)  44 us
    dot_general x5, matrix products, section_layer(): jnp.dot(normed, w_query, preferred_element_type=jnp.float32)  41.2 us
    ppermute x5, waiting for transfers between devices, collect(): theirs = lax.ppermute(grown, axis, [(d, d ^ reach) for d in range(ways)])  29.3 us
    all_to_all x2, starting transfers between devices, route_memory(): lax.all_to_all(outgoing, 'dp', split_axis=0, concat_axis=0, tiled=True)  11 us
  transfers between devices with their start and end apart: 20, of which 15 were waited for; matrix products, arithmetic and copies ran while one was open for 3% of the time, Pallas kernels for 0%

profile of v1, /device:TPU:0, one launch (start us, length us, event | category | flops | bytes accessed | tf_op | source)
XLA Modules:
  0.0 511.0 jit_solution(3795206162003100466)
XLA Ops:
  8.2 3.0 collective-permute-start
  12.2 10.9 %all-gather = bf16[1,64,4096]{2,1,0:T(8,128)(2,1)S(1)} all-gather(bf16[1,32,4096]{2,1,0:T(8,128)(2,1)S(1)} %slice_select_fusion), channel_id=2, replica_groups=mesh['phase'=2,'dp'=8,'mp'=2] {'mp'}, dimensions={1}, use_global_device_ids=true | all-gather | bytes 786432 | tf_op jit(solution)/shard_map/all_gather | solution.py:37
  23.4 1.4 fusion.256
  30.2 8.1 %fusion.85 = bf16[128,2048]{1,0:T(8,128)(2,1)S(1)} fusion(bf16[1,4096,2048]{2,1,0:T(8,128)(2,1)} %param.13, bf16[64,4096]{1,0:T(8,128)(2,1)S(1)} %get-tuple-element.52, bf16[64,4096]{1,0:T(8,128)(2,1)S(1)} %get-tuple-element.51), kind=kOutput, calls=%fused_computation.65 | convolution fusion | flops 2149842944 | bytes 18350080 | tf_op jit(solution)/shard_map/dot_general | solution.py:46
  38.7 2.9 fusion.140
  42.5 2.9 fusion.125
  46.7 8.8 %fusion.38 = bf16[2,32,4096]{2,1,0:T(8,128)(2,1)S(1)} fusion(bf16[2,32,2048]{2,1,0:T(8,128)(2,1)S(1)} %dot_general.132, bf16[1,2048,4096]{2,1,0:T(8,128)(2,1)} %param.16), kind=kOutput, calls=%fused_computation.36 | convolution fusion | flops 1074003968 | bytes 17563648 | tf_op jit(solution)/shard_map/dot_general | solution.py:79
  55.5 8.8 %fusion.35 = bf16[2,32,4096]{2,1,0:T(8,128)(2,1)S(1)} fusion(bf16[2,32,2048]{2,1,0:T(8,128)(2,1)S(1)} %dot_general.130, bf16[1,2048,4096]{2,1,0:T(8,128)(2,1)} %param.16), kind=kOutput, calls=%fused_computation.35 | convolution fusion | flops 1074003968 | bytes 17563648 | tf_op jit(solution)/shard_map/dot_general | solution.py:76
  65.4 9.3 %reduce-scatter.8.cloned.1.call-start = ((), (), s32[]{:S(2)}) async-start(), calls=%async_computation.8 | async-start | bytes 1572864 | tf_op jit(solution)/shard_map/reduce_scatter | solution.py:82
  74.7 12.7 %reduce-scatter.6.cloned.1.call-done = bf16[64,4096]{1,0:T(8,128)(2,1)} async-done(((bf16[128,4096]{1,0:T(8,128)(2,1)}), bf16[64,4096]{1,0:T(8,128)(2,1)}) %reduce-scatter.6.cloned.1.call-update) | async-done | bytes 524304 | tf_op jit(solution)/shard_map/reduce_scatter | solution.py:82
  87.4 1.1 convert_element_type.272
  90.6 8.9 %all_gather.16 = bf16[64,4096]{1,0:T(8,128)(2,1)S(1)} all-gather(bf16[32,4096]{1,0:T(8,128)(2,1)S(1)} %bitcast_select_fusion.9), channel_id=1, replica_groups=mesh['phase'=2,'dp'=8,'mp'=2] {'mp'}, dimensions={0}, use_global_device_ids=true | all-gather | bytes 786432 | tf_op jit(solution)/shard_map/all_gather | solution.py:37
  101.1 6.8 %collective-permute-done.3 = bf16[32,4096]{1,0:T(8,128)(2,1)S(1)} collective-permute-done((bf16[32,4096]{1,0:T(8,128)(2,1)S(1)}, bf16[32,4096]{1,0:T(8,128)(2,1)S(1)}, u32[]{:S(2)}, u32[]{:S(2)}) %collective-permute-start.3) | collective-permute-done | bytes 262176 | tf_op jit(solution)/shard_map/ppermute | solution.py:14
  108.5 8.3 %fusion.88 = bf16[128,2048]{1,0:T(8,128)(2,1)S(1)} fusion(bf16[1,4096,2048]{2,1,0:T(8,128)(2,1)} %param.13, bf16[64,4096]{1,0:T(8,128)(2,1)S(1)} %get-tuple-element.50, bf16[64,4096]{1,0:T(8,128)(2,1)S(1)} %get-tuple-element.49), kind=kOutput, calls=%fused_computation.66 | convolution fusion | flops 2149842944 | bytes 18350080 | tf_op jit(solution)/shard_map/dot_general | solution.py:46
  117.6 1.5 copy-done.23
  119.8 1.2 reshape.227
  121.0 1.5 fusion.307
  122.6 2.3 fusion.117
  124.9 2.8 fusion.121
  127.7 1.8 fusion.300
  129.9 8.8 %fusion.44 = bf16[2,32,4096]{2,1,0:T(8,128)(2,1)S(1)} fusion(bf16[2,32,2048]{2,1,0:T(8,128)(2,1)S(1)} %dot_general.141, bf16[1,2048,4096]{2,1,0:T(8,128)(2,1)} %param.16), kind=kOutput, calls=%fused_computation.38 | convolution fusion | flops 1074003968 | bytes 17563648 | tf_op jit(solution)/shard_map/dot_general | solution.py:79
  139.7 1.1 dot_general.139
  140.8 8.8 %fusion.41 = bf16[2,32,4096]{2,1,0:T(8,128)(2,1)S(1)} fusion(bf16[2,32,2048]{2,1,0:T(8,128)(2,1)S(1)} %dot_general.139, bf16[1,2048,4096]{2,1,0:T(8,128)(2,1)} %param.16), kind=kOutput, calls=%fused_computation.37 | convolution fusion | flops 1074003968 | bytes 17563648 | tf_op jit(solution)/shard_map/dot_general | solution.py:76
  150.8 20.5 %reduce-scatter.8.cloned.1.call-done = bf16[64,4096]{1,0:T(8,128)(2,1)} async-done(((bf16[128,4096]{1,0:T(8,128)(2,1)}), bf16[64,4096]{1,0:T(8,128)(2,1)}) %reduce-scatter.8.cloned.1.call-update) | async-done | bytes 524304 | tf_op jit(solution)/shard_map/reduce_scatter | solution.py:82
  171.3 1.1 convert_element_type.288
  173.3 1.1 fusion.258
  175.2 1.6 broadcast_select_fusion.1
  176.7 5.5 %all-to-all-start = ((bf16[8,32,4096]{2,1,0:T(8,128)(2,1)}), bf16[8,32,4096]{2,1,0:T(8,128)(2,1)S(1)}, u32[]{:S(2)}, u32[]{:S(2)}) async-start(bf16[8,32,4096]{2,1,0:T(8,128)(2,1)} %broadcast_select_fusion.1), calls=%async_computation.2 | async-start | bytes 4194304 | tf_op jit(solution)/shard_map/all_to_all | solution.py:102
  182.5 1.3 collective-permute-done.5
  185.5 7.8 %collective-permute-done.6 = bf16[32,4096]{1,0:T(8,128)(2,1)S(1)} collective-permute-done((bf16[32,4096]{1,0:T(8,128)(2,1)S(1)}, bf16[32,4096]{1,0:T(8,128)(2,1)S(1)}, u32[]{:S(2)}, u32[]{:S(2)}) %collective-permute-start.6) | collective-permute-done | bytes 262176 | tf_op jit(solution)/shard_map/ppermute | solution.py:14
  194.1 37.1 %all-to-all-done = bf16[8,32,4096]{2,1,0:T(8,128)(2,1)S(1)} async-done(((bf16[8,32,4096]{2,1,0:T(8,128)(2,1)}), bf16[8,32,4096]{2,1,0:T(8,128)(2,1)S(1)}, u32[]{:S(2)}, u32[]{:S(2)}) %all-to-all-start) | async-done | bytes 2097184 | tf_op jit(solution)/shard_map/all_to_all | solution.py:102
  233.2 8.2 %all_gather.17 = bf16[64,4096]{1,0:T(8,128)(2,1)S(1)} all-gather(bf16[32,4096]{1,0:T(8,128)(2,1)S(1)} %broadcast_select_fusion.5), channel_id=1, replica_groups=mesh['phase'=2,'dp'=8,'mp'=2] {'mp'}, dimensions={0}, use_global_device_ids=true | all-gather | bytes 786432 | tf_op jit(solution)/shard_map/all_gather | solution.py:37
  241.6 1.4 fusion.166
  243.0 8.3 %fusion.91 = bf16[128,2048]{1,0:T(8,128)(2,1)S(1)} fusion(bf16[1,4096,2048]{2,1,0:T(8,128)(2,1)} %param.13, bf16[64,4096]{1,0:T(8,128)(2,1)S(1)} %get-tuple-element.48, bf16[64,4096]{1,0:T(8,128)(2,1)S(1)} %get-tuple-element.47), kind=kOutput, calls=%fused_computation.67 | convolution fusion | flops 2149842944 | bytes 18350080 | tf_op jit(solution)/shard_map/dot_general | solution.py:46
  252.0 1.5 copy-done.24
  255.2 1.3 fusion.115
  256.5 2.0 fusion.122
  258.9 8.8 %fusion.50 = bf16[2,32,4096]{2,1,0:T(8,128)(2,1)S(1)} fusion(bf16[2,32,2048]{2,1,0:T(8,128)(2,1)S(1)} %dot_general.150, bf16[1,2048,4096]{2,1,0:T(8,128)(2,1)} %param.16), kind=kOutput, calls=%fused_computation.40 | convolution fusion | flops 1074003968 | bytes 17563648 | tf_op jit(solution)/shard_map/dot_general | solution.py:79
  268.1 8.8 %fusion.47 = bf16[2,32,4096]{2,1,0:T(8,128)(2,1)S(1)} fusion(bf16[2,32,2048]{2,1,0:T(8,128)(2,1)S(1)} %dot_general.148, bf16[1,2048,4096]{2,1,0:T(8,128)(2,1)} %param.16), kind=kOutput, calls=%fused_computation.39 | convolution fusion | flops 1074003968 | bytes 17563648 | tf_op jit(solution)/shard_map/dot_general | solution.py:76
  279.0 18.4 %reduce-scatter.10.cloned.1.call-done = bf16[64,4096]{1,0:T(8,128)(2,1)} async-done(((bf16[128,4096]{1,0:T(8,128)(2,1)}), bf16[64,4096]{1,0:T(8,128)(2,1)}) %reduce-scatter.10.cloned.1.call-update) | async-done | bytes 524304 | tf_op jit(solution)/shard_map/reduce_scatter | solution.py:82
  297.4 1.1 convert_element_type.304
  301.7 1.6 broadcast_select_fusion
  303.3 5.5 %all-to-all-start.1 = ((bf16[8,32,4096]{2,1,0:T(8,128)(2,1)}), bf16[8,32,4096]{2,1,0:T(8,128)(2,1)S(1)}, u32[]{:S(2)}, u32[]{:S(2)}) async-start(bf16[8,32,4096]{2,1,0:T(8,128)(2,1)} %broadcast_select_fusion), calls=%async_computation.4 | async-start | bytes 4194304 | tf_op jit(solution)/shard_map/all_to_all | solution.py:102
  309.0 1.5 collective-permute-done.8
  312.1 7.8 %collective-permute-done.9 = bf16[32,4096]{1,0:T(8,128)(2,1)S(1)} collective-permute-done((bf16[32,4096]{1,0:T(8,128)(2,1)S(1)}, bf16[32,4096]{1,0:T(8,128)(2,1)S(1)}, u32[]{:S(2)}, u32[]{:S(2)}) %collective-permute-start.9) | collective-permute-done | bytes 262176 | tf_op jit(solution)/shard_map/ppermute | solution.py:14
  320.6 36.8 %all-to-all-done.1 = bf16[8,32,4096]{2,1,0:T(8,128)(2,1)S(1)} async-done(((bf16[8,32,4096]{2,1,0:T(8,128)(2,1)}), bf16[8,32,4096]{2,1,0:T(8,128)(2,1)S(1)}, u32[]{:S(2)}, u32[]{:S(2)}) %all-to-all-start.1) | async-done | bytes 2097184 | tf_op jit(solution)/shard_map/all_to_all | solution.py:102
  360.1 7.9 %all_gather.18 = bf16[64,4096]{1,0:T(8,128)(2,1)S(1)} all-gather(bf16[32,4096]{1,0:T(8,128)(2,1)S(1)} %broadcast_select_fusion.4), channel_id=1, replica_groups=mesh['phase'=2,'dp'=8,'mp'=2] {'mp'}, dimensions={0}, use_global_device_ids=true | all-gather | bytes 786432 | tf_op jit(solution)/shard_map/all_gather | solution.py:37
  368.2 1.4 fusion.172
  369.6 8.3 %fusion.94 = bf16[128,2048]{1,0:T(8,128)(2,1)S(1)} fusion(bf16[1,4096,2048]{2,1,0:T(8,128)(2,1)} %param.13, bf16[64,4096]{1,0:T(8,128)(2,1)S(1)} %get-tuple-element.46, bf16[64,4096]{1,0:T(8,128)(2,1)S(1)} %get-tuple-element.45), kind=kOutput, calls=%fused_computation.68 | convolution fusion | flops 2149842944 | bytes 18350080 | tf_op jit(solution)/shard_map/dot_general | solution.py:46
  378.6 1.5 copy-done.25
  383.8 8.8 %fusion.56 = bf16[2,32,4096]{2,1,0:T(8,128)(2,1)S(1)} fusion(bf16[2,32,2048]{2,1,0:T(8,128)(2,1)S(1)} %dot_general.159, bf16[1,2048,4096]{2,1,0:T(8,128)(2,1)} %param.16), kind=kOutput, calls=%fused_computation.42 | convolution fusion | flops 1074003968 | bytes 17563648 | tf_op jit(solution)/shard_map/dot_general | solution.py:79
  393.7 9.0 %fusion.53 = bf16[2,32,4096]{2,1,0:T(8,128)(2,1)S(1)} fusion(bf16[2,32,2048]{2,1,0:T(8,128)(2,1)} %dot_general.157, bf16[1,2048,4096]{2,1,0:T(8,128)(2,1)} %param.16), kind=kOutput, calls=%fused_computation.41 | convolution fusion | flops 1074003968 | bytes 17563648 | tf_op jit(solution)/shard_map/dot_general | solution.py:76
  405.2 18.1 %reduce-scatter.12.cloned.1.call-done = bf16[64,4096]{1,0:T(8,128)(2,1)} async-done(((bf16[128,4096]{1,0:T(8,128)(2,1)}), bf16[64,4096]{1,0:T(8,128)(2,1)}) %reduce-scatter.12.cloned.1.call-update) | async-done | bytes 524304 | tf_op jit(solution)/shard_map/reduce_scatter | solution.py:82
  424.4 1.3 bitcast_dynamic-update-slice_fusion
  427.4 9.2 %all_gather.19 = bf16[64,4096]{1,0:T(8,128)(2,1)S(1)} all-gather(bf16[32,4096]{1,0:T(8,128)(2,1)S(1)} %broadcast_select_fusion.3), channel_id=1, replica_groups=mesh['phase'=2,'dp'=8,'mp'=2] {'mp'}, dimensions={0}, use_global_device_ids=true | all-gather | bytes 786432 | tf_op jit(solution)/shard_map/all_gather | solution.py:37
  437.3 6.9 %collective-permute-done.12 = bf16[32,4096]{1,0:T(8,128)(2,1)S(1)} collective-permute-done((bf16[32,4096]{1,0:T(8,128)(2,1)S(1)}, bf16[32,4096]{1,0:T(8,128)(2,1)S(1)}, u32[]{:S(2)}, u32[]{:S(2)}) %collective-permute-start.12) | collective-permute-done | bytes 262176 | tf_op jit(solution)/shard_map/ppermute | solution.py:14
  444.8 8.3 %fusion.97 = bf16[128,2048]{1,0:T(8,128)(2,1)S(1)} fusion(bf16[1,4096,2048]{2,1,0:T(8,128)(2,1)} %param.13, bf16[64,4096]{1,0:T(8,128)(2,1)S(1)} %get-tuple-element.44, bf16[64,4096]{1,0:T(8,128)(2,1)S(1)} %get-tuple-element.43), kind=kOutput, calls=%fused_computation.69 | convolution fusion | flops 2149842944 | bytes 18350080 | tf_op jit(solution)/shard_map/dot_general | solution.py:46
  453.9 1.5 copy-done.26
  457.0 1.3 fusion.111
  458.3 2.0 fusion.124
  460.8 8.8 %fusion.62 = bf16[2,32,4096]{2,1,0:T(8,128)(2,1)S(1)} fusion(bf16[2,32,2048]{2,1,0:T(8,128)(2,1)S(1)} %dot_general.168, bf16[1,2048,4096]{2,1,0:T(8,128)(2,1)} %param.16), kind=kOutput, calls=%fused_computation.44 | convolution fusion | flops 1074003968 | bytes 17563648 | tf_op jit(solution)/shard_map/dot_general | solution.py:79
  470.0 8.8 %fusion.59 = bf16[2,32,4096]{2,1,0:T(8,128)(2,1)S(1)} fusion(bf16[2,32,2048]{2,1,0:T(8,128)(2,1)S(1)} %dot_general.166, bf16[1,2048,4096]{2,1,0:T(8,128)(2,1)} %param.16), kind=kOutput, calls=%fused_computation.43 | convolution fusion | flops 1074003968 | bytes 17563648 | tf_op jit(solution)/shard_map/dot_general | solution.py:76
  480.7 19.7 %reduce-scatter.14.cloned.1.call-done = bf16[64,4096]{1,0:T(8,128)(2,1)} async-done(((bf16[128,4096]{1,0:T(8,128)(2,1)}), bf16[64,4096]{1,0:T(8,128)(2,1)}) %reduce-scatter.14.cloned.1.call-update) | async-done | bytes 524304 | tf_op jit(solution)/shard_map/reduce_scatter | solution.py:82
  501.5 1.2 fusion.205
  (196 shorter events, 59.3 us)
Async XLA Ops:
  7.2 80.2 %reduce-scatter.6.cloned.1.call-start = ((), (), s32[]{:S(2)}) async-start(), calls=%async_computation.7 | async-start | bytes 1572864 | tf_op jit(solution)/shard_map/reduce_scatter | solution.py:82
  8.2 21.4 %collective-permute-start = (bf16[32,4096]{1,0:T(8,128)(2,1)S(1)}, bf16[32,4096]{1,0:T(8,128)(2,1)S(1)}, u32[]{:S(2)}, u32[]{:S(2)}) collective-permute-start(bf16[32,4096]{1,0:T(8,128)(2,1)S(1)} %select_bitcast_fusion), channel_id=1, source_target_pairs={{0,1},{1,0},{2,3},{3,2},{4,5},{5,4},{6,7},{7,6},{8,9},{9,8},{10,11... | collective-permute-start | bytes 786440 | tf_op jit(solution)/shard_map/ppermute | solution.py:14
  64.3 24.3 %copy-start.5 = (bf16[2,32,4096]{2,1,0:T(8,128)(2,1)S(1)}, bf16[2,32,4096]{2,1,0:T(8,128)(2,1)}, u32[]{:S(2)}) copy-start(bf16[2,32,4096]{2,1,0:T(8,128)(2,1)} %param.10) | copy-start | bytes 1572868
  65.4 105.9 %reduce-scatter.8.cloned.1.call-start = ((), (), s32[]{:S(2)}) async-start(), calls=%async_computation.8 | async-start | bytes 1572864 | tf_op jit(solution)/shard_map/reduce_scatter | solution.py:82
  88.7 1.8 collective-permute-start.1
  90.0 9.5 %collective-permute-start.2 = (bf16[32,4096]{1,0:T(8,128)(2,1)S(1)}, bf16[32,4096]{1,0:T(8,128)(2,1)S(1)}, u32[]{:S(2)}, u32[]{:S(2)}) collective-permute-start(bf16[32,4096]{1,0:T(8,128)(2,1)S(1)} %get-tuple-element.16), channel_id=1, source_target_pairs={{0,16},{16,0},{1,17},{17,1},{2,18},{18,2},{3,19},{19,3},{4,20},{20... | collective-permute-start | bytes 786440 | tf_op jit(solution)/shard_map/ppermute | solution.py:25
  100.5 7.4 %collective-permute-start.3 = (bf16[32,4096]{1,0:T(8,128)(2,1)S(1)}, bf16[32,4096]{1,0:T(8,128)(2,1)S(1)}, u32[]{:S(2)}, u32[]{:S(2)}) collective-permute-start(bf16[32,4096]{1,0:T(8,128)(2,1)S(1)} %bitcast_select_fusion.8), channel_id=1, source_target_pairs={{0,1},{1,0},{2,3},{3,2},{4,5},{5,4},{6,7},{7,6},{8,9},{9,8},{10,11... | collective-permute-start | bytes 786440 | tf_op jit(solution)/shard_map/ppermute | solution.py:14
  108.5 8.4 %copy-start.19 = (bf16[1,4096,512]{2,1,0:T(8,128)(2,1)S(1)}, bf16[1,4096,512]{2,1,0:T(8,128)(2,1)}, u32[]{:S(2)}) copy-start(bf16[1,4096,512]{2,1,0:T(8,128)(2,1)} %param.14) | copy-start | bytes 12582916
  116.9 2.2 copy-start.23
  129.9 8.9 %copy-start.10 = (bf16[64,4,4,128]{3,0,2,1:T(8,128)(2,1)S(1)}, bf16[64,4,4,128]{3,0,2,1:T(8,128)(2,1)}, u32[]{:S(2)}) copy-start(bf16[64,4,4,128]{3,0,2,1:T(8,128)(2,1)} %get-tuple-element.39) | copy-start | bytes 786436
  149.6 23.7 %copy-start.18 = (s32[2,8]{1,0:T(2,128)S(1)}, s32[2,8]{1,0:T(2,128)}, u32[]{:S(2)}) copy-start(s32[2,8]{1,0:T(2,128)} %param.12) | copy-start | bytes 196
  173.3 3.4 copy-start.1
  173.3 1.8 collective-permute-start.4
  175.1 1.6 copy-start.8
  176.7 54.4 %all-to-all-start = ((bf16[8,32,4096]{2,1,0:T(8,128)(2,1)}), bf16[8,32,4096]{2,1,0:T(8,128)(2,1)S(1)}, u32[]{:S(2)}, u32[]{:S(2)}) async-start(bf16[8,32,4096]{2,1,0:T(8,128)(2,1)} %broadcast_select_fusion.1), calls=%async_computation.2 | async-start | bytes 4194304 | tf_op jit(solution)/shard_map/all_to_all | solution.py:102
  182.2 115.1 %reduce-scatter.10.cloned.1.call-start = ((), (), s32[]{:S(2)}) async-start(), calls=%async_computation.9 | async-start | bytes 1572864 | tf_op jit(solution)/shard_map/reduce_scatter | solution.py:82
  182.3 1.6 collective-permute-start.5
  184.9 8.5 %collective-permute-start.6 = (bf16[32,4096]{1,0:T(8,128)(2,1)S(1)}, bf16[32,4096]{1,0:T(8,128)(2,1)S(1)}, u32[]{:S(2)}, u32[]{:S(2)}) collective-permute-start(bf16[32,4096]{1,0:T(8,128)(2,1)S(1)} %bitcast_select_fusion.6), channel_id=1, source_target_pairs={{0,1},{1,0},{2,3},{3,2},{4,5},{5,4},{6,7},{7,6},{8,9},{9,8},{10,11... | collective-permute-start | bytes 786440 | tf_op jit(solution)/shard_map/ppermute | solution.py:14
  193.4 0.7 copy-start.7
  243.0 8.3 %copy-start.20 = (bf16[1,4096,512]{2,1,0:T(8,128)(2,1)S(1)}, bf16[1,4096,512]{2,1,0:T(8,128)(2,1)}, u32[]{:S(2)}) copy-start(bf16[1,4096,512]{2,1,0:T(8,128)(2,1)} %param.14) | copy-start | bytes 12582916
  251.3 2.2 copy-start.24
  253.5 1.2 copy-start.17
  299.5 9.4 %copy-start.14 = (bf16[32,4096]{1,0:T(8,128)(2,1)S(1)}, bf16[32,4096]{1,0:T(8,128)(2,1)}, u32[]{:S(2)}) copy-start(bf16[32,4096]{1,0:T(8,128)(2,1)} %get-tuple-element.12) | copy-start | bytes 786436
  299.5 1.5 collective-permute-start.7
  301.0 0.7 copy-start.9
  303.3 54.1 %all-to-all-start.1 = ((bf16[8,32,4096]{2,1,0:T(8,128)(2,1)}), bf16[8,32,4096]{2,1,0:T(8,128)(2,1)S(1)}, u32[]{:S(2)}, u32[]{:S(2)}) async-start(bf16[8,32,4096]{2,1,0:T(8,128)(2,1)} %broadcast_select_fusion), calls=%async_computation.4 | async-start | bytes 4194304 | tf_op jit(solution)/shard_map/all_to_all | solution.py:102
  308.8 114.5 %reduce-scatter.12.cloned.1.call-start = ((), (), s32[]{:S(2)}) async-start(), calls=%async_computation.10 | async-start | bytes 1572864 | tf_op jit(solution)/shard_map/reduce_scatter | solution.py:82
  308.9 1.6 collective-permute-start.8
  311.5 8.4 %collective-permute-start.9 = (bf16[32,4096]{1,0:T(8,128)(2,1)S(1)}, bf16[32,4096]{1,0:T(8,128)(2,1)S(1)}, u32[]{:S(2)}, u32[]{:S(2)}) collective-permute-start(bf16[32,4096]{1,0:T(8,128)(2,1)S(1)} %bitcast_select_fusion.4), channel_id=1, source_target_pairs={{0,1},{1,0},{2,3},{3,2},{4,5},{5,4},{6,7},{7,6},{8,9},{9,8},{10,11... | collective-permute-start | bytes 786440 | tf_op jit(solution)/shard_map/ppermute | solution.py:14
  319.9 0.7 copy-start.6
  359.4 0.7 copy-start.4
  369.6 8.3 %copy-start.21 = (bf16[1,4096,512]{2,1,0:T(8,128)(2,1)S(1)}, bf16[1,4096,512]{2,1,0:T(8,128)(2,1)}, u32[]{:S(2)}) copy-start(bf16[1,4096,512]{2,1,0:T(8,128)(2,1)} %param.14) | copy-start | bytes 12582916
  377.9 2.2 copy-start.25
  380.1 1.2 copy-start.16
  393.7 10.8 %copy-start.2 = (bf16[4,32,4096]{2,1,0:T(8,128)(2,1)S(1)}, bf16[4,32,4096]{2,1,0:T(8,128)(2,1)}, u32[]{:S(2)}) copy-start(bf16[4,32,4096]{2,1,0:T(8,128)(2,1)} %get-tuple-element.29) | copy-start | bytes 3145732
  403.7 96.7 %reduce-scatter.14.cloned.1.call-start = ((), (), s32[]{:S(2)}) async-start(), calls=%async_computation.11 | async-start | bytes 1572864 | tf_op jit(solution)/shard_map/reduce_scatter | solution.py:82
  425.8 1.6 collective-permute-start.10
  425.8 10.8 %collective-permute-start.11 = (bf16[32,4096]{1,0:T(8,128)(2,1)S(1)}, bf16[32,4096]{1,0:T(8,128)(2,1)S(1)}, u32[]{:S(2)}, u32[]{:S(2)}) collective-permute-start(bf16[32,4096]{1,0:T(8,128)(2,1)S(1)} %get-tuple-element.10), channel_id=1, source_target_pairs={{0,16},{16,0},{1,17},{17,1},{2,18},{18,2},{3,19},{19,3},{4,20},{20... | collective-permute-start | bytes 786440 | tf_op jit(solution)/shard_map/ppermute | solution.py:25
  427.4 9.3 %copy-start.11 = (bf16[32,4096]{1,0:T(8,128)(2,1)}, bf16[32,4096]{1,0:T(8,128)(2,1)S(1)}, u32[]{:S(2)}) copy-start(bf16[32,4096]{1,0:T(8,128)(2,1)S(1)} %collective-permute-done.10) | copy-start | bytes 786436
  436.6 7.8 %copy-start.13 = (bf16[32,4096]{1,0:T(8,128)(2,1)}, bf16[32,4096]{1,0:T(8,128)(2,1)S(1)}, u32[]{:S(2)}) copy-start(bf16[32,4096]{1,0:T(8,128)(2,1)S(1)} %collective-permute-done.11) | copy-start | bytes 786436
  436.7 7.6 %collective-permute-start.12 = (bf16[32,4096]{1,0:T(8,128)(2,1)S(1)}, bf16[32,4096]{1,0:T(8,128)(2,1)S(1)}, u32[]{:S(2)}, u32[]{:S(2)}) collective-permute-start(bf16[32,4096]{1,0:T(8,128)(2,1)S(1)} %broadcast_select_fusion.2), channel_id=1, source_target_pairs={{0,1},{1,0},{2,3},{3,2},{4,5},{5,4},{6,7},{7,6},{8,9},{9,8},{10,11... | collective-permute-start | bytes 786440 | tf_op jit(solution)/shard_map/ppermute | solution.py:14
  444.8 8.3 %copy-start.22 = (bf16[1,4096,512]{2,1,0:T(8,128)(2,1)S(1)}, bf16[1,4096,512]{2,1,0:T(8,128)(2,1)}, u32[]{:S(2)}) copy-start(bf16[1,4096,512]{2,1,0:T(8,128)(2,1)} %param.14) | copy-start | bytes 12582916
  453.1 2.2 copy-start.26
  455.3 1.2 copy-start.15
  478.8 22.8 %copy-start.12 = (bf16[32,4096]{1,0:T(8,128)(2,1)S(1)}, bf16[32,4096]{1,0:T(8,128)(2,1)}, u32[]{:S(2)}) copy-start(bf16[32,4096]{1,0:T(8,128)(2,1)} %copy-done.11) | copy-start | bytes 786436
  502.8 1.0 copy-start
  502.8 1.3 copy-start.3
Sparse Core Ops, SparseCore 0:
  65.5 21.8 reduce-scatter.5
  150.8 20.3 reduce-scatter.7
  278.1 19.2 reduce-scatter.9
  403.8 19.4 reduce-scatter.11
  480.0 20.3 reduce-scatter.13
